TPU v7x, 32 devices: a whole 2x2x4 slice. The times are simulated.
32 devices in a mesh: snap: 16 (over z, y, core), zone: 2 (over x).
Axes of the slice: x: 2, y: 2, z: 4, core: 2. Of those that a mesh axis runs over, the one named last changes fastest.
Arguments:
- forward: bfloat16 [2048, 2048], P('zone', 'snap'), may hold values from -40 to 40, as said below
- adjoint: bfloat16 [2048, 2048], P('zone', 'snap'), may hold values from -0.125 to 0.125
Outputs:
- rotated: float32 [2048, 2048], P('snap', 'zone')
Inputs may be any that keep to these rules, and one draw needn't show every extreme that they name: `forward`: independent entries, each snapshot column with its own scale.
All inputs are finite; a program needn't handle non-finite values.
Results may differ from a plain program's by a relative error of at most 0.0003.
Values may be sent and summed in bfloat16 or wider, within the bound.
A program may use at most 64 MiB of HBM per device.

v0:
```python
import jax
import jax.numpy as jnp
from jax import lax
from jax.sharding import PartitionSpec as P

ROUNDS = 8


def shifted(value, axis, steps):
    count = lax.axis_size(axis)
    initial, last = (max(0, -steps), min(count, count - steps))
    return lax.ppermute(value, axis, [(source, source + steps) for source in range(initial, last)])


def highdot(a, b):
    return jnp.dot(a, b, precision=lax.Precision.HIGHEST, preferred_element_type=jnp.float32)


def pair_gram(pair):
    local = lax.dot_general(
        pair,
        pair,
        (((1,), (1,)), ((), ())),
        precision=lax.Precision.HIGHEST,
        preferred_element_type=jnp.float32,
    )
    return local


def orthogonalize(pair):
    gram = pair_gram(pair)
    scales = jnp.sqrt(jnp.diagonal(gram) + 1e-06)
    corr = gram / (scales[:, None] * scales[None, :])
    half_rows = corr.shape[0] // 2
    block = corr[:half_rows, half_rows:]
    spread = jnp.sqrt(jnp.sum(block * block))
    coupling = 0.5 * block / jnp.maximum(spread, 1.0)
    zeros = jnp.zeros((half_rows, half_rows), jnp.float32)
    skew = jnp.concatenate(
        [jnp.concatenate([zeros, coupling], axis=1), jnp.concatenate([-coupling.T, zeros], axis=1)],
        axis=0,
    )
    ident = jnp.eye(corr.shape[0], dtype=jnp.float32)
    minus = ident - skew
    square = highdot(minus, minus)
    normal = ident + highdot(skew.T, skew)
    factor = jnp.linalg.cholesky(normal)
    middle = lax.linalg.triangular_solve(factor, square, left_side=True, lower=True)
    rotation = lax.linalg.triangular_solve(
        factor, middle, left_side=True, lower=True, transpose_a=True
    )
    return highdot(rotation, pair)


def shards(forward, adjoint):
    partial_rows = lax.dot_general(
        forward,
        lax.all_gather(adjoint, "snap", axis=1, tiled=True),
        (((0,), (0,)), ((), ())),
        preferred_element_type=jnp.float32,
    )
    rows = lax.psum(partial_rows, "zone")
    half_rows = rows.shape[0] // 2
    top = rows[:half_rows]
    bottom = rows[half_rows:]
    place = lax.axis_index("snap")
    final_place = lax.axis_size("snap") - 1
    for rnd in range(ROUNDS):
        done = orthogonalize(jnp.concatenate([top, bottom], axis=0))
        top = done[:half_rows]
        bottom = done[half_rows:]
        if rnd + 1 < ROUNDS:
            outgoing = jnp.where(place == 0, bottom, top)
            came_right = shifted(outgoing, "snap", 1)
            came_left = shifted(bottom, "snap", -1)
            new_top = jnp.where(place == 0, top, came_right)
            new_bottom = jnp.where(place == final_place, top, came_left)
            top = new_top
            bottom = new_bottom
    result = jnp.concatenate([top, bottom], axis=0)
    width = result.shape[1] // lax.axis_size("zone")
    result = lax.dynamic_slice_in_dim(result, lax.axis_index("zone") * width, width, 1)
    return result


def solution(mesh):
    return jax.shard_map(
        shards,
        mesh=mesh,
        in_specs=(P("zone", "snap"), P("zone", "snap")),
        out_specs=P("snap", "zone"),
        check_vma=False,
    )
```

profile of v0, /device:TPU:1, one launch (start us, length us, event | category | flops | bytes accessed | tf_op | source)
XLA Modules:
  0.0 462.8 jit_solution(3175419123350176471)
XLA Ops:
  7.3 58.0 %all-gather.2.cloned.1.call-done = bf16[1024,2048]{1,0:T(8,128)(2,1)} async-done(((bf16[1024,128]{1,0:T(8,128)(2,1)}), bf16[1024,2048]{1,0:T(8,128)(2,1)}) %all-gather.2.cloned.1.call-update) | async-done | bytes 4194320 | tf_op jit(solution)/shard_map/all_gather | solution.py:58
  69.2 37.9 %all-reduce.18.cloned.1.call-done = f32[128,2048]{1,0:T(8,128)} async-done(((f32[128,2048]{1,0:T(8,128)}), f32[128,2048]{1,0:T(8,128)}) %all-reduce.18.cloned.1.call-update) | async-done | bytes 1048592 | tf_op jit(solution)/shard_map/psum | solution.py:62
  113.5 11.7 %cholesky.134 = f32[128,128]{1,0:T(8,128)S(1)} custom-call(f32[128,128]{1,0:T(8,128)S(1)} %fusion.69), custom_call_target="Cholesky" | custom-call | tf_op jit(solution)/shard_map/jit(cholesky)/cholesky | solution.py:47
  126.6 9.8 %custom-call.39 = f32[1,128,128]{1,2,0:T(8,128)S(1)} custom-call(f32[1,128,128]{2,1,0:T(8,128)S(1)} %fusion.14), custom_call_target="InvertDiagBlocksLowerTriangular" | custom-call | tf_op jit(solution)/shard_map/triangular_solve/custom-call.2 | solution.py:49
  143.8 9.6 %collective-permute-done = f32[64,2048]{1,0:T(8,128)S(1)} collective-permute-done((f32[64,2048]{1,0:T(8,128)S(1)}, f32[64,2048]{1,0:T(8,128)S(1)}, u32[]{:S(2)}, u32[]{:S(2)}) %collective-permute-start) | collective-permute-done | bytes 524320 | tf_op jit(solution)/shard_map/ppermute | solution.py:12
  158.3 11.7 %cholesky.145 = f32[128,128]{1,0:T(8,128)S(1)} custom-call(f32[128,128]{1,0:T(8,128)S(1)} %fusion.64), custom_call_target="Cholesky" | custom-call | tf_op jit(solution)/shard_map/jit(cholesky)/cholesky | solution.py:47
  171.3 9.8 %custom-call.41 = f32[1,128,128]{1,2,0:T(8,128)S(1)} custom-call(f32[1,128,128]{2,1,0:T(8,128)S(1)} %fusion.15), custom_call_target="InvertDiagBlocksLowerTriangular" | custom-call | tf_op jit(solution)/shard_map/triangular_solve/custom-call.2 | solution.py:49
  189.3 9.6 %collective-permute-done.2 = f32[64,2048]{1,0:T(8,128)S(1)} collective-permute-done((f32[64,2048]{1,0:T(8,128)S(1)}, f32[64,2048]{1,0:T(8,128)S(1)}, u32[]{:S(2)}, u32[]{:S(2)}) %collective-permute-start.2) | collective-permute-done | bytes 524320 | tf_op jit(solution)/shard_map/ppermute | solution.py:12
  203.7 11.7 %cholesky.156 = f32[128,128]{1,0:T(8,128)S(1)} custom-call(f32[128,128]{1,0:T(8,128)S(1)} %fusion.59), custom_call_target="Cholesky" | custom-call | tf_op jit(solution)/shard_map/jit(cholesky)/cholesky | solution.py:47
  216.8 9.8 %custom-call.43 = f32[1,128,128]{1,2,0:T(8,128)S(1)} custom-call(f32[1,128,128]{2,1,0:T(8,128)S(1)} %fusion.16), custom_call_target="InvertDiagBlocksLowerTriangular" | custom-call | tf_op jit(solution)/shard_map/triangular_solve/custom-call.2 | solution.py:49
  234.9 9.4 %collective-permute-done.4 = f32[64,2048]{1,0:T(8,128)S(1)} collective-permute-done((f32[64,2048]{1,0:T(8,128)S(1)}, f32[64,2048]{1,0:T(8,128)S(1)}, u32[]{:S(2)}, u32[]{:S(2)}) %collective-permute-start.4) | collective-permute-done | bytes 524320 | tf_op jit(solution)/shard_map/ppermute | solution.py:12
  249.1 11.7 %cholesky.167 = f32[128,128]{1,0:T(8,128)S(1)} custom-call(f32[128,128]{1,0:T(8,128)S(1)} %fusion.54), custom_call_target="Cholesky" | custom-call | tf_op jit(solution)/shard_map/jit(cholesky)/cholesky | solution.py:47
  262.2 9.8 %custom-call.45 = f32[1,128,128]{1,2,0:T(8,128)S(1)} custom-call(f32[1,128,128]{2,1,0:T(8,128)S(1)} %fusion.17), custom_call_target="InvertDiagBlocksLowerTriangular" | custom-call | tf_op jit(solution)/shard_map/triangular_solve/custom-call.2 | solution.py:49
  280.1 9.6 %collective-permute-done.6 = f32[64,2048]{1,0:T(8,128)S(1)} collective-permute-done((f32[64,2048]{1,0:T(8,128)S(1)}, f32[64,2048]{1,0:T(8,128)S(1)}, u32[]{:S(2)}, u32[]{:S(2)}) %collective-permute-start.6) | collective-permute-done | bytes 524320 | tf_op jit(solution)/shard_map/ppermute | solution.py:12
  294.6 11.7 %cholesky.178 = f32[128,128]{1,0:T(8,128)S(1)} custom-call(f32[128,128]{1,0:T(8,128)S(1)} %fusion.49), custom_call_target="Cholesky" | custom-call | tf_op jit(solution)/shard_map/jit(cholesky)/cholesky | solution.py:47
  307.6 9.8 %custom-call.47 = f32[1,128,128]{1,2,0:T(8,128)S(1)} custom-call(f32[1,128,128]{2,1,0:T(8,128)S(1)} %fusion.18), custom_call_target="InvertDiagBlocksLowerTriangular" | custom-call | tf_op jit(solution)/shard_map/triangular_solve/custom-call.2 | solution.py:49
  325.6 9.6 %collective-permute-done.8 = f32[64,2048]{1,0:T(8,128)S(1)} collective-permute-done((f32[64,2048]{1,0:T(8,128)S(1)}, f32[64,2048]{1,0:T(8,128)S(1)}, u32[]{:S(2)}, u32[]{:S(2)}) %collective-permute-start.8) | collective-permute-done | bytes 524320 | tf_op jit(solution)/shard_map/ppermute | solution.py:12
  340.0 11.7 %cholesky.189 = f32[128,128]{1,0:T(8,128)S(1)} custom-call(f32[128,128]{1,0:T(8,128)S(1)} %fusion.44), custom_call_target="Cholesky" | custom-call | tf_op jit(solution)/shard_map/jit(cholesky)/cholesky | solution.py:47
  353.1 9.8 %custom-call.49 = f32[1,128,128]{1,2,0:T(8,128)S(1)} custom-call(f32[1,128,128]{2,1,0:T(8,128)S(1)} %fusion.19), custom_call_target="InvertDiagBlocksLowerTriangular" | custom-call | tf_op jit(solution)/shard_map/triangular_solve/custom-call.2 | solution.py:49
  371.2 9.4 %collective-permute-done.10 = f32[64,2048]{1,0:T(8,128)S(1)} collective-permute-done((f32[64,2048]{1,0:T(8,128)S(1)}, f32[64,2048]{1,0:T(8,128)S(1)}, u32[]{:S(2)}, u32[]{:S(2)}) %collective-permute-start.10) | collective-permute-done | bytes 524320 | tf_op jit(solution)/shard_map/ppermute | solution.py:12
  385.5 11.7 %cholesky.200 = f32[128,128]{1,0:T(8,128)S(1)} custom-call(f32[128,128]{1,0:T(8,128)S(1)} %fusion.39), custom_call_target="Cholesky" | custom-call | tf_op jit(solution)/shard_map/jit(cholesky)/cholesky | solution.py:47
  398.5 9.8 %custom-call.51 = f32[1,128,128]{1,2,0:T(8,128)S(1)} custom-call(f32[1,128,128]{2,1,0:T(8,128)S(1)} %fusion.20), custom_call_target="InvertDiagBlocksLowerTriangular" | custom-call | tf_op jit(solution)/shard_map/triangular_solve/custom-call.2 | solution.py:49
  430.5 11.7 %cholesky.211 = f32[128,128]{1,0:T(8,128)S(1)} custom-call(f32[128,128]{1,0:T(8,128)S(1)} %fusion.34), custom_call_target="Cholesky" | custom-call | tf_op jit(solution)/shard_map/jit(cholesky)/cholesky | solution.py:47
  443.6 9.8 %custom-call.53 = f32[1,128,128]{1,2,0:T(8,128)S(1)} custom-call(f32[1,128,128]{2,1,0:T(8,128)S(1)} %fusion.21), custom_call_target="InvertDiagBlocksLowerTriangular" | custom-call | tf_op jit(solution)/shard_map/triangular_solve/custom-call.2 | solution.py:49
  (183 shorter events, 117.5 us)
Async XLA Ops:
  6.5 58.7 %copy-start = (bf16[1024,128]{1,0:T(8,128)(2,1)S(1)}, bf16[1024,128]{1,0:T(8,128)(2,1)}, u32[]{:S(2)}) copy-start(bf16[1024,128]{1,0:T(8,128)(2,1)} %param.7) | copy-start | bytes 786436
  6.5 58.7 %all-gather.2.cloned.1.call-start = ((), (), s32[]{:S(2)}) async-start(), calls=%async_computation | async-start | bytes 4456448 | tf_op jit(solution)/shard_map/all_gather | solution.py:58
  7.3 99.9 %all-reduce.18.cloned.1.call-start = ((), (), s32[]{:S(2)}) async-start(), calls=%async_computation.1 | async-start | bytes 2097152 | tf_op jit(solution)/shard_map/psum | solution.py:62
  107.2 29.7 %copy-start.1 = (f32[128,2048]{1,0:T(8,128)S(1)}, f32[128,2048]{1,0:T(8,128)}, u32[]{:S(2)}) copy-start(f32[128,2048]{1,0:T(8,128)} %all-reduce.18.cloned.1.call-done) | copy-start | bytes 3145732
  138.0 15.4 %collective-permute-start = (f32[64,2048]{1,0:T(8,128)S(1)}, f32[64,2048]{1,0:T(8,128)S(1)}, u32[]{:S(2)}, u32[]{:S(2)}) collective-permute-start(f32[64,2048]{1,0:T(8,128)S(1)} %get-tuple-element.50), channel_id=1, source_target_pairs={{0,2},{2,4},{4,6},{6,8},{8,10},{10,12},{12,14},{14,16},{16,18},{18... | collective-permute-start | bytes 1572872 | tf_op jit(solution)/shard_map/ppermute | solution.py:12
  141.7 11.7 %collective-permute-start.1 = (f32[64,2048]{1,0:T(8,128)S(1)}, f32[64,2048]{1,0:T(8,128)S(1)}, u32[]{:S(2)}, u32[]{:S(2)}) collective-permute-start(f32[64,2048]{1,0:T(8,128)S(1)} %get-tuple-element.51), channel_id=1, source_target_pairs={{2,0},{4,2},{6,4},{8,6},{10,8},{12,10},{14,12},{16,14},{18,16},{20... | collective-permute-start | bytes 1572872 | tf_op jit(solution)/shard_map/ppermute | solution.py:12
  182.7 16.1 %collective-permute-start.2 = (f32[64,2048]{1,0:T(8,128)S(1)}, f32[64,2048]{1,0:T(8,128)S(1)}, u32[]{:S(2)}, u32[]{:S(2)}) collective-permute-start(f32[64,2048]{1,0:T(8,128)S(1)} %get-tuple-element.46), channel_id=1, source_target_pairs={{0,2},{2,4},{4,6},{6,8},{8,10},{10,12},{12,14},{14,16},{16,18},{18... | collective-permute-start | bytes 1572872 | tf_op jit(solution)/shard_map/ppermute | solution.py:12
  187.1 11.7 %collective-permute-start.3 = (f32[64,2048]{1,0:T(8,128)S(1)}, f32[64,2048]{1,0:T(8,128)S(1)}, u32[]{:S(2)}, u32[]{:S(2)}) collective-permute-start(f32[64,2048]{1,0:T(8,128)S(1)} %get-tuple-element.47), channel_id=1, source_target_pairs={{2,0},{4,2},{6,4},{8,6},{10,8},{12,10},{14,12},{16,14},{18,16},{20... | collective-permute-start | bytes 1572872 | tf_op jit(solution)/shard_map/ppermute | solution.py:12
  228.2 16.1 %collective-permute-start.4 = (f32[64,2048]{1,0:T(8,128)S(1)}, f32[64,2048]{1,0:T(8,128)S(1)}, u32[]{:S(2)}, u32[]{:S(2)}) collective-permute-start(f32[64,2048]{1,0:T(8,128)S(1)} %get-tuple-element.42), channel_id=1, source_target_pairs={{0,2},{2,4},{4,6},{6,8},{8,10},{10,12},{12,14},{14,16},{16,18},{18... | collective-permute-start | bytes 1572872 | tf_op jit(solution)/shard_map/ppermute | solution.py:12
  232.6 11.7 %collective-permute-start.5 = (f32[64,2048]{1,0:T(8,128)S(1)}, f32[64,2048]{1,0:T(8,128)S(1)}, u32[]{:S(2)}, u32[]{:S(2)}) collective-permute-start(f32[64,2048]{1,0:T(8,128)S(1)} %get-tuple-element.43), channel_id=1, source_target_pairs={{2,0},{4,2},{6,4},{8,6},{10,8},{12,10},{14,12},{16,14},{18,16},{20... | collective-permute-start | bytes 1572872 | tf_op jit(solution)/shard_map/ppermute | solution.py:12
  273.6 16.1 %collective-permute-start.6 = (f32[64,2048]{1,0:T(8,128)S(1)}, f32[64,2048]{1,0:T(8,128)S(1)}, u32[]{:S(2)}, u32[]{:S(2)}) collective-permute-start(f32[64,2048]{1,0:T(8,128)S(1)} %get-tuple-element.38), channel_id=1, source_target_pairs={{0,2},{2,4},{4,6},{6,8},{8,10},{10,12},{12,14},{14,16},{16,18},{18... | collective-permute-start | bytes 1572872 | tf_op jit(solution)/shard_map/ppermute | solution.py:12
  278.0 11.7 %collective-permute-start.7 = (f32[64,2048]{1,0:T(8,128)S(1)}, f32[64,2048]{1,0:T(8,128)S(1)}, u32[]{:S(2)}, u32[]{:S(2)}) collective-permute-start(f32[64,2048]{1,0:T(8,128)S(1)} %get-tuple-element.39), channel_id=1, source_target_pairs={{2,0},{4,2},{6,4},{8,6},{10,8},{12,10},{14,12},{16,14},{18,16},{20... | collective-permute-start | bytes 1572872 | tf_op jit(solution)/shard_map/ppermute | solution.py:12
  319.1 16.1 %collective-permute-start.8 = (f32[64,2048]{1,0:T(8,128)S(1)}, f32[64,2048]{1,0:T(8,128)S(1)}, u32[]{:S(2)}, u32[]{:S(2)}) collective-permute-start(f32[64,2048]{1,0:T(8,128)S(1)} %get-tuple-element.34), channel_id=1, source_target_pairs={{0,2},{2,4},{4,6},{6,8},{8,10},{10,12},{12,14},{14,16},{16,18},{18... | collective-permute-start | bytes 1572872 | tf_op jit(solution)/shard_map/ppermute | solution.py:12
  323.5 11.7 %collective-permute-start.9 = (f32[64,2048]{1,0:T(8,128)S(1)}, f32[64,2048]{1,0:T(8,128)S(1)}, u32[]{:S(2)}, u32[]{:S(2)}) collective-permute-start(f32[64,2048]{1,0:T(8,128)S(1)} %get-tuple-element.35), channel_id=1, source_target_pairs={{2,0},{4,2},{6,4},{8,6},{10,8},{12,10},{14,12},{16,14},{18,16},{20... | collective-permute-start | bytes 1572872 | tf_op jit(solution)/shard_map/ppermute | solution.py:12
  364.5 16.1 %collective-permute-start.10 = (f32[64,2048]{1,0:T(8,128)S(1)}, f32[64,2048]{1,0:T(8,128)S(1)}, u32[]{:S(2)}, u32[]{:S(2)}) collective-permute-start(f32[64,2048]{1,0:T(8,128)S(1)} %get-tuple-element.30), channel_id=1, source_target_pairs={{0,2},{2,4},{4,6},{6,8},{8,10},{10,12},{12,14},{14,16},{16,18},{18... | collective-permute-start | bytes 1572872 | tf_op jit(solution)/shard_map/ppermute | solution.py:12
  368.9 11.7 %collective-permute-start.11 = (f32[64,2048]{1,0:T(8,128)S(1)}, f32[64,2048]{1,0:T(8,128)S(1)}, u32[]{:S(2)}, u32[]{:S(2)}) collective-permute-start(f32[64,2048]{1,0:T(8,128)S(1)} %get-tuple-element.31), channel_id=1, source_target_pairs={{2,0},{4,2},{6,4},{8,6},{10,8},{12,10},{14,12},{16,14},{18,16},{20... | collective-permute-start | bytes 1572872 | tf_op jit(solution)/shard_map/ppermute | solution.py:12
  410.0 15.7 %collective-permute-start.12 = (f32[64,2048]{1,0:T(8,128)S(1)}, f32[64,2048]{1,0:T(8,128)S(1)}, u32[]{:S(2)}, u32[]{:S(2)}) collective-permute-start(f32[64,2048]{1,0:T(8,128)S(1)} %get-tuple-element.26), channel_id=1, source_target_pairs={{0,2},{2,4},{4,6},{6,8},{8,10},{10,12},{12,14},{14,16},{16,18},{18... | collective-permute-start | bytes 1572872 | tf_op jit(solution)/shard_map/ppermute | solution.py:12
  414.4 11.4 %collective-permute-start.13 = (f32[64,2048]{1,0:T(8,128)S(1)}, f32[64,2048]{1,0:T(8,128)S(1)}, u32[]{:S(2)}, u32[]{:S(2)}) collective-permute-start(f32[64,2048]{1,0:T(8,128)S(1)} %get-tuple-element.27), channel_id=1, source_target_pairs={{2,0},{4,2},{6,4},{8,6},{10,8},{12,10},{14,12},{16,14},{18,16},{20... | collective-permute-start | bytes 1572872 | tf_op jit(solution)/shard_map/ppermute | solution.py:12
Sparse Core Ops, SparseCore 0:
  9.5 55.7 all-gather.1
  69.3 37.7 all-reduce.17
where the time goes:
time: 471 us; the launch traced here: 463 us
  other arithmetic  191 us (41%)
  waiting for transfers between devices  163 us (35%)
  starting transfers between devices  45.3 us (10%)
  matrix products  31.1 us (7%)
  between operations  20.1 us (4%)
  local copies, waits for them, and re-layouts  12.7 us (3%)
    another operation x24, other arithmetic, orthogonalize(): factor = jnp.linalg.cholesky(normal)  99.1 us
    another operation x16, other arithmetic, orthogonalize(): lax.linalg.triangular_solve(factor, middle, left_side=True, lower=True, t...  83.7 us
    ppermute x14, waiting for transfers between devices, shifted(): lax.ppermute(value, axis, [(source, source + steps) for source in range(i...  66.4 us
    all_gather x1, waiting for transfers between devices, shards(): lax.all_gather(adjoint, 'snap', axis=1, tiled=True)  58 us
    ppermute x14, starting transfers between devices, shifted(): lax.ppermute(value, axis, [(source, source + steps) for source in range(i...  45.2 us
    psum x1, waiting for transfers between devices, shards(): rows = lax.psum(partial_rows, 'zone')  37.9 us
    dot_general x24, matrix products, highdot(): jnp.dot(a, b, precision=lax.Precision.HIGHEST, preferred_element_type=jnp...  13.8 us
    gather x8, local copies, waits for them, and re-layouts, orthogonalize(): scales = jnp.sqrt(jnp.diagonal(gram) + 1e-06)  9.96 us
  transfers between devices with their start and end apart: 16, of which 9 were waited for; matrix products, arithmetic and copies ran while one was open for 0% of the time, Pallas kernels for 0%

commit v1 on v0

--- a/solution.py
+++ b/solution.py
@@ -4,6 +4,18 @@
 from jax.sharding import PartitionSpec as P
 
 ROUNDS = 8
+
+
+def collect(value, axis, dim):
+    ways, here = (lax.axis_size(axis), lax.axis_index(axis))
+    grown, reach = (value, 1)
+    while reach < ways:
+        theirs = lax.ppermute(grown, axis, [(d, d ^ reach) for d in range(ways)])
+        mine_first = jnp.concatenate([grown, theirs], axis=dim)
+        theirs_first = jnp.concatenate([theirs, grown], axis=dim)
+        grown = jnp.where(here & reach == 0, mine_first, theirs_first)
+        reach = 2 * reach
+    return grown
 
 
 def shifted(value, axis, steps):
@@ -55,7 +67,7 @@
 def shards(forward, adjoint):
     partial_rows = lax.dot_general(
         forward,
-        lax.all_gather(adjoint, "snap", axis=1, tiled=True),
+        collect(adjoint, "snap", 1),
         (((0,), (0,)), ((), ())),
         preferred_element_type=jnp.float32,
     )

time: 471 us -> 554 us (1.18)
  waiting for transfers between devices: 163 us -> 237 us
    ppermute x0 -> x4, waiting for transfers between devices: none -> 127 us  [collect(): theirs = lax.ppermute(grown, axis, [(d, d ^ reach) for d in range(ways)])]
    all_gather x1 -> x0, waiting for transfers between devices: 58 us -> none  [shards(): lax.all_gather(adjoint, 'snap', axis=1, tiled=True)]
    ppermute x0 -> x4, starting transfers between devices: none -> 5.69 us  [collect(): theirs = lax.ppermute(grown, axis, [(d, d ^ reach) for d in range(ways)])]
  transfers between devices with their start and end apart: 16 -> 19, of which waited for: 9 -> 12; matrix products, arithmetic and copies ran while one was open for 0% -> 0% of each run, Pallas kernels for 0% -> 0%
where the time goes in v1:
time: 554 us; the launch traced here: 550 us
  waiting for transfers between devices  237 us (43%)
  other arithmetic  195 us (35%)
  starting transfers between devices  49.1 us (9%)
  matrix products  33.2 us (6%)
  between operations  20.1 us (4%)
  local copies, waits for them, and re-layouts  15 us (3%)
    ppermute x4, waiting for transfers between devices, collect(): theirs = lax.ppermute(grown, axis, [(d, d ^ reach) for d in range(ways)])  127 us
    another operation x24, other arithmetic, orthogonalize(): factor = jnp.linalg.cholesky(normal)  99.1 us
    another operation x16, other arithmetic, orthogonalize(): lax.linalg.triangular_solve(factor, middle, left_side=True, lower=True, t...  83.7 us
    ppermute x14, waiting for transfers between devices, shifted(): lax.ppermute(value, axis, [(source, source + steps) for source in range(i...  68.3 us
    ppermute x14, starting transfers between devices, shifted(): lax.ppermute(value, axis, [(source, source + steps) for source in range(i...  43.4 us
    psum x1, waiting for transfers between devices, shards(): rows = lax.psum(partial_rows, 'zone')  41.3 us
    dot_general x24, matrix products, highdot(): jnp.dot(a, b, precision=lax.Precision.HIGHEST, preferred_element_type=jnp...  13.8 us
    gather x8, local copies, waits for them, and re-layouts, orthogonalize(): scales = jnp.sqrt(jnp.diagonal(gram) + 1e-06)  12.2 us
  transfers between devices with their start and end apart: 19, of which 12 were waited for; matrix products, arithmetic and copies ran while one was open for 0% of the time, Pallas kernels for 0%

profile of v1, /device:TPU:1, one launch (start us, length us, event | category | flops | bytes accessed | tf_op | source)
XLA Modules:
  0.0 549.8 jit_solution(8094256436768628550)
XLA Ops:
  11.9 12.0 %collective-permute-done.1 = bf16[1024,256]{1,0:T(8,128)(2,1)S(1)} collective-permute-done((bf16[1024,256]{1,0:T(8,128)(2,1)S(1)}, bf16[1024,256]{1,0:T(8,128)(2,1)S(1)}, u32[]{:S(2)}, u32[]{:S(2)}) %collective-permute-start.1) | collective-permute-done | bytes 524320 | tf_op jit(solution)/shard_map/ppermute | solution.py:13
  25.4 22.7 %collective-permute-done.2 = bf16[1024,512]{1,0:T(8,128)(2,1)} collective-permute-done((bf16[1024,512]{1,0:T(8,128)(2,1)S(1)}, bf16[1024,512]{1,0:T(8,128)(2,1)}, u32[]{:S(2)}, u32[]{:S(2)}) %collective-permute-start.2) | collective-permute-done | bytes 1048608 | tf_op jit(solution)/shard_map/ppermute | solution.py:13
  52.3 91.0 %collective-permute-done.3 = bf16[1024,1024]{1,0:T(8,128)(2,1)} collective-permute-done((bf16[1024,1024]{1,0:T(8,128)(2,1)S(1)}, bf16[1024,1024]{1,0:T(8,128)(2,1)}, u32[]{:S(2)}, u32[]{:S(2)}) %collective-permute-start.3) | collective-permute-done | bytes 2097184 | tf_op jit(solution)/shard_map/ppermute | solution.py:13
  148.6 41.3 %all-reduce.18.cloned.1.call-done = f32[128,2048]{0,1:T(8,128)} async-done(((f32[128,2048]{0,1:T(8,128)}), f32[128,2048]{0,1:T(8,128)}) %all-reduce.18.cloned.1.call-update) | async-done | bytes 1048592 | tf_op jit(solution)/shard_map/psum | solution.py:74
  197.6 11.7 %cholesky.134 = f32[128,128]{1,0:T(8,128)S(1)} custom-call(f32[128,128]{1,0:T(8,128)S(1)} %fusion.77), custom_call_target="Cholesky" | custom-call | tf_op jit(solution)/shard_map/jit(cholesky)/cholesky | solution.py:59
  210.6 9.8 %custom-call.39 = f32[1,128,128]{1,2,0:T(8,128)S(1)} custom-call(f32[1,128,128]{2,1,0:T(8,128)S(1)} %fusion.22), custom_call_target="InvertDiagBlocksLowerTriangular" | custom-call | tf_op jit(solution)/shard_map/triangular_solve/custom-call.2 | solution.py:61
  243.6 11.7 %cholesky.145 = f32[128,128]{1,0:T(8,128)S(1)} custom-call(f32[128,128]{1,0:T(8,128)S(1)} %fusion.72), custom_call_target="Cholesky" | custom-call | tf_op jit(solution)/shard_map/jit(cholesky)/cholesky | solution.py:59
  256.6 9.8 %custom-call.41 = f32[1,128,128]{1,2,0:T(8,128)S(1)} custom-call(f32[1,128,128]{2,1,0:T(8,128)S(1)} %fusion.23), custom_call_target="InvertDiagBlocksLowerTriangular" | custom-call | tf_op jit(solution)/shard_map/triangular_solve/custom-call.2 | solution.py:61
  274.4 9.8 %collective-permute-done.6 = f32[64,2048]{1,0:T(8,128)S(1)} collective-permute-done((f32[64,2048]{1,0:T(8,128)S(1)}, f32[64,2048]{1,0:T(8,128)S(1)}, u32[]{:S(2)}, u32[]{:S(2)}) %collective-permute-start.6) | collective-permute-done | bytes 524320 | tf_op jit(solution)/shard_map/ppermute | solution.py:24
  289.2 11.7 %cholesky.156 = f32[128,128]{1,0:T(8,128)S(1)} custom-call(f32[128,128]{1,0:T(8,128)S(1)} %fusion.67), custom_call_target="Cholesky" | custom-call | tf_op jit(solution)/shard_map/jit(cholesky)/cholesky | solution.py:59
  302.3 9.8 %custom-call.43 = f32[1,128,128]{1,2,0:T(8,128)S(1)} custom-call(f32[1,128,128]{2,1,0:T(8,128)S(1)} %fusion.24), custom_call_target="InvertDiagBlocksLowerTriangular" | custom-call | tf_op jit(solution)/shard_map/triangular_solve/custom-call.2 | solution.py:61
  320.0 9.8 %collective-permute-done.8 = f32[64,2048]{1,0:T(8,128)S(1)} collective-permute-done((f32[64,2048]{1,0:T(8,128)S(1)}, f32[64,2048]{1,0:T(8,128)S(1)}, u32[]{:S(2)}, u32[]{:S(2)}) %collective-permute-start.8) | collective-permute-done | bytes 524320 | tf_op jit(solution)/shard_map/ppermute | solution.py:24
  335.1 11.7 %cholesky.167 = f32[128,128]{1,0:T(8,128)S(1)} custom-call(f32[128,128]{1,0:T(8,128)S(1)} %fusion.62), custom_call_target="Cholesky" | custom-call | tf_op jit(solution)/shard_map/jit(cholesky)/cholesky | solution.py:59
  348.1 9.8 %custom-call.45 = f32[1,128,128]{1,2,0:T(8,128)S(1)} custom-call(f32[1,128,128]{2,1,0:T(8,128)S(1)} %fusion.25), custom_call_target="InvertDiagBlocksLowerTriangular" | custom-call | tf_op jit(solution)/shard_map/triangular_solve/custom-call.2 | solution.py:61
  365.9 9.8 %collective-permute-done.10 = f32[64,2048]{1,0:T(8,128)S(1)} collective-permute-done((f32[64,2048]{1,0:T(8,128)S(1)}, f32[64,2048]{1,0:T(8,128)S(1)}, u32[]{:S(2)}, u32[]{:S(2)}) %collective-permute-start.10) | collective-permute-done | bytes 524320 | tf_op jit(solution)/shard_map/ppermute | solution.py:24
  380.7 11.7 %cholesky.178 = f32[128,128]{1,0:T(8,128)S(1)} custom-call(f32[128,128]{1,0:T(8,128)S(1)} %fusion.57), custom_call_target="Cholesky" | custom-call | tf_op jit(solution)/shard_map/jit(cholesky)/cholesky | solution.py:59
  393.7 9.8 %custom-call.47 = f32[1,128,128]{1,2,0:T(8,128)S(1)} custom-call(f32[1,128,128]{2,1,0:T(8,128)S(1)} %fusion.26), custom_call_target="InvertDiagBlocksLowerTriangular" | custom-call | tf_op jit(solution)/shard_map/triangular_solve/custom-call.2 | solution.py:61
  411.5 9.8 %collective-permute-done.12 = f32[64,2048]{1,0:T(8,128)S(1)} collective-permute-done((f32[64,2048]{1,0:T(8,128)S(1)}, f32[64,2048]{1,0:T(8,128)S(1)}, u32[]{:S(2)}, u32[]{:S(2)}) %collective-permute-start.12) | collective-permute-done | bytes 524320 | tf_op jit(solution)/shard_map/ppermute | solution.py:24
  426.3 11.7 %cholesky.189 = f32[128,128]{1,0:T(8,128)S(1)} custom-call(f32[128,128]{1,0:T(8,128)S(1)} %fusion.52), custom_call_target="Cholesky" | custom-call | tf_op jit(solution)/shard_map/jit(cholesky)/cholesky | solution.py:59
  439.4 9.8 %custom-call.49 = f32[1,128,128]{1,2,0:T(8,128)S(1)} custom-call(f32[1,128,128]{2,1,0:T(8,128)S(1)} %fusion.27), custom_call_target="InvertDiagBlocksLowerTriangular" | custom-call | tf_op jit(solution)/shard_map/triangular_solve/custom-call.2 | solution.py:61
  472.2 11.7 %cholesky.200 = f32[128,128]{1,0:T(8,128)S(1)} custom-call(f32[128,128]{1,0:T(8,128)S(1)} %fusion.47), custom_call_target="Cholesky" | custom-call | tf_op jit(solution)/shard_map/jit(cholesky)/cholesky | solution.py:59
  485.2 9.8 %custom-call.51 = f32[1,128,128]{1,2,0:T(8,128)S(1)} custom-call(f32[1,128,128]{2,1,0:T(8,128)S(1)} %fusion.28), custom_call_target="InvertDiagBlocksLowerTriangular" | custom-call | tf_op jit(solution)/shard_map/triangular_solve/custom-call.2 | solution.py:61
  517.5 11.7 %cholesky.211 = f32[128,128]{1,0:T(8,128)S(1)} custom-call(f32[128,128]{1,0:T(8,128)S(1)} %fusion.42), custom_call_target="Cholesky" | custom-call | tf_op jit(solution)/shard_map/jit(cholesky)/cholesky | solution.py:59
  530.5 9.8 %custom-call.53 = f32[1,128,128]{1,2,0:T(8,128)S(1)} custom-call(f32[1,128,128]{2,1,0:T(8,128)S(1)} %fusion.29), custom_call_target="InvertDiagBlocksLowerTriangular" | custom-call | tf_op jit(solution)/shard_map/triangular_solve/custom-call.2 | solution.py:61
  (191 shorter events, 151.3 us)
Async XLA Ops:
  6.5 136.8 %copy-start = (bf16[1024,128]{1,0:T(8,128)(2,1)S(1)}, bf16[1024,128]{1,0:T(8,128)(2,1)}, u32[]{:S(2)}) copy-start(bf16[1024,128]{1,0:T(8,128)(2,1)} %param.7) | copy-start | bytes 786436
  6.5 183.4 %all-reduce.18.cloned.1.call-start = ((), (), s32[]{:S(2)}) async-start(), calls=%async_computation | async-start | bytes 2097152 | tf_op jit(solution)/shard_map/psum | solution.py:74
  6.5 1.7 collective-permute-start
  9.5 14.4 %collective-permute-start.1 = (bf16[1024,256]{1,0:T(8,128)(2,1)S(1)}, bf16[1024,256]{1,0:T(8,128)(2,1)S(1)}, u32[]{:S(2)}, u32[]{:S(2)}) collective-permute-start(bf16[1024,256]{1,0:T(8,128)(2,1)S(1)} %maximum_select_fusion.6), channel_id=1, source_target_pairs={{0,4},{2,6},{4,0},{6,2},{8,12},{10,14},{12,8},{14,10},{16,20},{18,... | collective-permute-start | bytes 1572872 | tf_op jit(solution)/shard_map/ppermute | solution.py:13
  24.2 24.0 %collective-permute-start.2 = (bf16[1024,512]{1,0:T(8,128)(2,1)S(1)}, bf16[1024,512]{1,0:T(8,128)(2,1)}, u32[]{:S(2)}, u32[]{:S(2)}) collective-permute-start(bf16[1024,512]{1,0:T(8,128)(2,1)S(1)} %maximum_select_fusion.5), channel_id=1, source_target_pairs={{0,8},{2,10},{4,12},{6,14},{8,0},{10,2},{12,4},{14,6},{16,24},{18,... | collective-permute-start | bytes 3145736 | tf_op jit(solution)/shard_map/ppermute | solution.py:13
  50.4 92.9 %collective-permute-start.3 = (bf16[1024,1024]{1,0:T(8,128)(2,1)S(1)}, bf16[1024,1024]{1,0:T(8,128)(2,1)}, u32[]{:S(2)}, u32[]{:S(2)}) collective-permute-start(bf16[1024,1024]{1,0:T(8,128)(2,1)S(1)} %maximum_select_fusion.4), channel_id=1, source_target_pairs={{0,16},{2,18},{4,20},{6,22},{8,24},{10,26},{12,28},{14,30},{16,0},... | collective-permute-start | bytes 6291464 | tf_op jit(solution)/shard_map/ppermute | solution.py:13
  189.9 31.1 %copy-start.1 = (f32[128,2048]{0,1:T(8,128)S(1)}, f32[128,2048]{0,1:T(8,128)}, u32[]{:S(2)}) copy-start(f32[128,2048]{0,1:T(8,128)} %all-reduce.18.cloned.1.call-done) | copy-start | bytes 3145732
  222.1 15.4 %collective-permute-start.4 = (f32[64,2048]{1,0:T(8,128)S(1)}, f32[64,2048]{1,0:T(8,128)S(1)}, u32[]{:S(2)}, u32[]{:S(2)}) collective-permute-start(f32[64,2048]{1,0:T(8,128)S(1)} %get-tuple-element.50), channel_id=1, source_target_pairs={{0,2},{2,4},{4,6},{6,8},{8,10},{10,12},{12,14},{14,16},{16,18},{18... | collective-permute-start | bytes 1572872 | tf_op jit(solution)/shard_map/ppermute | solution.py:24
  225.8 11.7 %collective-permute-start.5 = (f32[64,2048]{1,0:T(8,128)S(1)}, f32[64,2048]{1,0:T(8,128)}, u32[]{:S(2)}, u32[]{:S(2)}) collective-permute-start(f32[64,2048]{1,0:T(8,128)S(1)} %get-tuple-element.51), channel_id=1, source_target_pairs={{2,0},{4,2},{6,4},{8,6},{10,8},{12,10},{14,12},{16,14},{18,16},{20... | collective-permute-start | bytes 1572872 | tf_op jit(solution)/shard_map/ppermute | solution.py:24
  268.1 16.1 %collective-permute-start.6 = (f32[64,2048]{1,0:T(8,128)S(1)}, f32[64,2048]{1,0:T(8,128)S(1)}, u32[]{:S(2)}, u32[]{:S(2)}) collective-permute-start(f32[64,2048]{1,0:T(8,128)S(1)} %get-tuple-element.46), channel_id=1, source_target_pairs={{0,2},{2,4},{4,6},{6,8},{8,10},{10,12},{12,14},{14,16},{16,18},{18... | collective-permute-start | bytes 1572872 | tf_op jit(solution)/shard_map/ppermute | solution.py:24
  272.5 11.7 %collective-permute-start.7 = (f32[64,2048]{1,0:T(8,128)S(1)}, f32[64,2048]{1,0:T(8,128)S(1)}, u32[]{:S(2)}, u32[]{:S(2)}) collective-permute-start(f32[64,2048]{1,0:T(8,128)S(1)} %get-tuple-element.47), channel_id=1, source_target_pairs={{2,0},{4,2},{6,4},{8,6},{10,8},{12,10},{14,12},{16,14},{18,16},{20... | collective-permute-start | bytes 1572872 | tf_op jit(solution)/shard_map/ppermute | solution.py:24
  313.7 16.1 %collective-permute-start.8 = (f32[64,2048]{1,0:T(8,128)S(1)}, f32[64,2048]{1,0:T(8,128)S(1)}, u32[]{:S(2)}, u32[]{:S(2)}) collective-permute-start(f32[64,2048]{1,0:T(8,128)S(1)} %get-tuple-element.42), channel_id=1, source_target_pairs={{0,2},{2,4},{4,6},{6,8},{8,10},{10,12},{12,14},{14,16},{16,18},{18... | collective-permute-start | bytes 1572872 | tf_op jit(solution)/shard_map/ppermute | solution.py:24
  318.1 11.7 %collective-permute-start.9 = (f32[64,2048]{1,0:T(8,128)S(1)}, f32[64,2048]{1,0:T(8,128)S(1)}, u32[]{:S(2)}, u32[]{:S(2)}) collective-permute-start(f32[64,2048]{1,0:T(8,128)S(1)} %get-tuple-element.43), channel_id=1, source_target_pairs={{2,0},{4,2},{6,4},{8,6},{10,8},{12,10},{14,12},{16,14},{18,16},{20... | collective-permute-start | bytes 1572872 | tf_op jit(solution)/shard_map/ppermute | solution.py:24
  359.6 16.1 %collective-permute-start.10 = (f32[64,2048]{1,0:T(8,128)S(1)}, f32[64,2048]{1,0:T(8,128)S(1)}, u32[]{:S(2)}, u32[]{:S(2)}) collective-permute-start(f32[64,2048]{1,0:T(8,128)S(1)} %get-tuple-element.38), channel_id=1, source_target_pairs={{0,2},{2,4},{4,6},{6,8},{8,10},{10,12},{12,14},{14,16},{16,18},{18... | collective-permute-start | bytes 1572872 | tf_op jit(solution)/shard_map/ppermute | solution.py:24
  364.0 11.7 %collective-permute-start.11 = (f32[64,2048]{1,0:T(8,128)S(1)}, f32[64,2048]{1,0:T(8,128)S(1)}, u32[]{:S(2)}, u32[]{:S(2)}) collective-permute-start(f32[64,2048]{1,0:T(8,128)S(1)} %get-tuple-element.39), channel_id=1, source_target_pairs={{2,0},{4,2},{6,4},{8,6},{10,8},{12,10},{14,12},{16,14},{18,16},{20... | collective-permute-start | bytes 1572872 | tf_op jit(solution)/shard_map/ppermute | solution.py:24
  405.2 16.1 %collective-permute-start.12 = (f32[64,2048]{1,0:T(8,128)S(1)}, f32[64,2048]{1,0:T(8,128)S(1)}, u32[]{:S(2)}, u32[]{:S(2)}) collective-permute-start(f32[64,2048]{1,0:T(8,128)S(1)} %get-tuple-element.34), channel_id=1, source_target_pairs={{0,2},{2,4},{4,6},{6,8},{8,10},{10,12},{12,14},{14,16},{16,18},{18... | collective-permute-start | bytes 1572872 | tf_op jit(solution)/shard_map/ppermute | solution.py:24
  409.6 11.7 %collective-permute-start.13 = (f32[64,2048]{1,0:T(8,128)S(1)}, f32[64,2048]{1,0:T(8,128)S(1)}, u32[]{:S(2)}, u32[]{:S(2)}) collective-permute-start(f32[64,2048]{1,0:T(8,128)S(1)} %get-tuple-element.35), channel_id=1, source_target_pairs={{2,0},{4,2},{6,4},{8,6},{10,8},{12,10},{14,12},{16,14},{18,16},{20... | collective-permute-start | bytes 1572872 | tf_op jit(solution)/shard_map/ppermute | solution.py:24
  450.8 16.1 %collective-permute-start.14 = (f32[64,2048]{1,0:T(8,128)S(1)}, f32[64,2048]{1,0:T(8,128)S(1)}, u32[]{:S(2)}, u32[]{:S(2)}) collective-permute-start(f32[64,2048]{1,0:T(8,128)S(1)} %get-tuple-element.30), channel_id=1, source_target_pairs={{0,2},{2,4},{4,6},{6,8},{8,10},{10,12},{12,14},{14,16},{16,18},{18... | collective-permute-start | bytes 1572872 | tf_op jit(solution)/shard_map/ppermute | solution.py:24
  455.2 11.7 %collective-permute-start.15 = (f32[64,2048]{1,0:T(8,128)S(1)}, f32[64,2048]{1,0:T(8,128)S(1)}, u32[]{:S(2)}, u32[]{:S(2)}) collective-permute-start(f32[64,2048]{1,0:T(8,128)S(1)} %get-tuple-element.31), channel_id=1, source_target_pairs={{2,0},{4,2},{6,4},{8,6},{10,8},{12,10},{14,12},{16,14},{18,16},{20... | collective-permute-start | bytes 1572872 | tf_op jit(solution)/shard_map/ppermute | solution.py:24
  496.7 15.8 %collective-permute-start.16 = (f32[64,2048]{1,0:T(8,128)S(1)}, f32[64,2048]{1,0:T(8,128)S(1)}, u32[]{:S(2)}, u32[]{:S(2)}) collective-permute-start(f32[64,2048]{1,0:T(8,128)S(1)} %get-tuple-element.26), channel_id=1, source_target_pairs={{0,2},{2,4},{4,6},{6,8},{8,10},{10,12},{12,14},{14,16},{16,18},{18... | collective-permute-start | bytes 1572872 | tf_op jit(solution)/shard_map/ppermute | solution.py:24
  501.1 11.4 %collective-permute-start.17 = (f32[64,2048]{1,0:T(8,128)S(1)}, f32[64,2048]{1,0:T(8,128)S(1)}, u32[]{:S(2)}, u32[]{:S(2)}) collective-permute-start(f32[64,2048]{1,0:T(8,128)S(1)} %get-tuple-element.27), channel_id=1, source_target_pairs={{2,0},{4,2},{6,4},{8,6},{10,8},{12,10},{14,12},{16,14},{18,16},{20... | collective-permute-start | bytes 1572872 | tf_op jit(solution)/shard_map/ppermute | solution.py:24
Sparse Core Ops, SparseCore 0:
  148.7 41.1 all-reduce.17
